TPU v7x, 32 devices: a whole 2x2x4 slice. The times are simulated.
32 devices in a mesh: dp: 8 (over z, y), expert: 4 (over x, core).
Axes of the slice: x: 2, y: 2, z: 4, core: 2. Of those that a mesh axis runs over, the one named last changes fastest.
Arguments:
- tokens: bfloat16 [12288, 768], P(('dp', 'expert')), may hold values from -6 to 6
- groups: int32 [32, 384], P(('dp', 'expert')), may hold values from 0 to 1, never falling along the last dimension, each value on 1 to 261 neighbouring positions
- key_mask: int32 [12288], P(('dp', 'expert')), may hold values 0 or 1
- routes: int32 [12288, 1], P(('dp', 'expert')), may hold values from 0 to 2; in each aligned block of 384 rows (0 to 383, 384 to 767, ...) at most 144 rows name the same one
- query_weight: bfloat16 [2, 768, 768], P(None, ('dp', 'expert')), may hold values from -0.21875 to 0.21875
- key_weight: bfloat16 [2, 768, 768], P(None, ('dp', 'expert')), may hold values from -0.21875 to 0.21875
- value_weight: bfloat16 [2, 768, 768], P(None, ('dp', 'expert')), may hold values from -0.21875 to 0.21875
- output_weight: bfloat16 [2, 768, 768], P(None, ('dp', 'expert')), may hold values from -1.75 to 1.75
- norm_first: bfloat16 [2, 768], P(None, ('dp', 'expert')), may hold values from 0.25 to 1.75
- norm_second: bfloat16 [2, 768], P(None, ('dp', 'expert')), may hold values from 0.25 to 1.75
- expert_in: bfloat16 [2, 3, 768, 3072], P(None, None, 'dp', 'expert'), may hold values from -0.21875 to 0.21875
- expert_out: bfloat16 [2, 3, 3072, 768], P(None, None, 'expert', 'dp'), may hold values from -0.109375 to 0.109375
- cotangent: float32 [12288, 768], P(('dp', 'expert')), may hold values from -6 to 6
Outputs:
- mixed: bfloat16 [12288, 768], P(('dp', 'expert'))
- delta_tokens: float32 [12288, 768], P(('dp', 'expert'))
- delta_query: float32 [2, 768, 768], P(None, ('dp', 'expert'))
- delta_key: float32 [2, 768, 768], P(None, ('dp', 'expert'))
- delta_value: float32 [2, 768, 768], P(None, ('dp', 'expert'))
- delta_output: float32 [2, 768, 768], P(None, ('dp', 'expert'))
- delta_first: float32 [2, 768], P(None, ('dp', 'expert'))
- delta_second: float32 [2, 768], P(None, ('dp', 'expert'))
- delta_in: float32 [2, 3, 768, 3072], P(None, None, 'dp', 'expert')
- delta_out: float32 [2, 3, 3072, 768], P(None, None, 'expert', 'dp')
Inputs may be any that keep to these rules, and one draw needn't show every extreme that they name: Each device's block holds 2 groups numbered in order, each of 1 to 261 tokens. `routes`: among the 384 tokens of one device no expert is named more than 144 times; on some devices one expert is named exactly 144 times.
All inputs are finite; a program needn't handle non-finite values. No bound on the sum of `key_mask` on one device may be relied on, other than what follows from the above.
Results may differ from a plain program's by a relative error of at most 0.024.
Values may be sent and summed in bfloat16 or wider, within the bound.
No kernel may reach another device: no remote copies, remote signals or barrier semaphores. Data moves between devices by JAX's collectives and lax.ppermute only.
A program may use at most 256 MiB of HBM per device.

v0:
```python
from functools import partial
import jax
import jax.numpy as jnp
from jax import lax
from jax.sharding import PartitionSpec as P

HEADS = 12
HEAD_DIM = 64
EXPERTS = 3
LAYERS = 2
MOST = 144
epsilon = 1e-05
score_scale = 0.125


def layer_norm(values, gain_vector):
    average = jnp.mean(values, -1, keepdims=True)
    centered = values - average
    spread = jnp.mean(centered * centered, -1, keepdims=True)
    return centered * lax.rsqrt(spread + epsilon) * gain_vector


def contract_rows(left, right):
    return lax.dot_general(
        left, right, (((0,), (0,)), ((), ())), preferred_element_type=jnp.float32
    )


def contract_cols(left, right):
    return lax.dot_general(
        left, right, (((1,), (1,)), ((), ())), preferred_element_type=jnp.float32
    )


def slot_tables(route_row):
    row_count = route_row.shape[0]
    one_hot = (route_row[:, None] == jnp.arange(EXPERTS, dtype=jnp.int32)[None, :]).astype(
        jnp.int32
    )
    running = jnp.cumsum(one_hot, 0) - 1
    position = jnp.sum(running * one_hot, 1)
    slot_of = route_row * MOST + position
    token_of = (
        jnp.zeros((EXPERTS * MOST,), jnp.int32)
        .at[slot_of]
        .set(jnp.arange(row_count, dtype=jnp.int32))
    )
    filled = jnp.zeros((EXPERTS * MOST,), jnp.int32).at[slot_of].set(1)
    return (slot_of, token_of, filled)


def allowed_pairs(group_row, mask_row):
    row_count = group_row.shape[0]
    same_group = group_row[:, None] == group_row[None, :]
    diagonal = jnp.arange(row_count)[:, None] == jnp.arange(row_count)[None, :]
    return same_group & ((mask_row[None, :] == 1) | diagonal)


def head_slice(matrix, head_index):
    return lax.dynamic_slice_in_dim(matrix, head_index * HEAD_DIM, HEAD_DIM, 1)


def join_heads(stacked):
    return jnp.transpose(stacked, (1, 0, 2)).reshape(stacked.shape[1], HEADS * HEAD_DIM)


def attend_forward(query_rows, key_rows, value_rows, allowed):

    def one_head(head_index):
        query_head = head_slice(query_rows, head_index)
        key_head = head_slice(key_rows, head_index)
        value_head = head_slice(value_rows, head_index)
        scores = contract_cols(query_head, key_head) * score_scale
        scores = jnp.where(allowed, scores, -1e30)
        highest = jnp.max(scores, 1, keepdims=True)
        powers = jnp.exp(scores - highest)
        totals = jnp.sum(powers, 1, keepdims=True)
        probs = (powers / totals).astype(jnp.bfloat16)
        context = jnp.dot(probs, value_head, preferred_element_type=jnp.float32)
        return (context, (highest + jnp.log(totals))[:, 0])

    contexts, log_totals = lax.map(one_head, jnp.arange(HEADS, dtype=jnp.int32))
    return (join_heads(contexts), log_totals)


def attend_backward(query_rows, key_rows, value_rows, allowed, log_totals, context_grad):

    def one_head(head_index):
        query_head = head_slice(query_rows, head_index)
        key_head = head_slice(key_rows, head_index)
        value_head = head_slice(value_rows, head_index)
        grad_head = head_slice(context_grad, head_index)
        scores = contract_cols(query_head, key_head) * score_scale
        probs = jnp.where(allowed, jnp.exp(scores - log_totals[head_index][:, None]), 0.0)
        prob_grad = contract_cols(grad_head, value_head)
        inner = jnp.sum(probs * prob_grad, 1, keepdims=True)
        score_grad = (probs * (prob_grad - inner)).astype(jnp.bfloat16)
        query_grad = score_scale * jnp.dot(score_grad, key_head, preferred_element_type=jnp.float32)
        key_grad = score_scale * contract_rows(score_grad, query_head)
        value_grad = contract_rows(probs.astype(jnp.bfloat16), grad_head)
        return (query_grad, key_grad, value_grad)

    parts = lax.map(one_head, jnp.arange(HEADS, dtype=jnp.int32))
    return tuple((join_heads(part).astype(jnp.bfloat16) for part in parts))


def layer_forward(inputs, allowed, tables, attention, experts_full):
    query_weight, key_weight, value_weight, output_weight, first_gain, second_gain = attention
    weight_in, weight_out = experts_full
    width = inputs.shape[1]
    normed = layer_norm(inputs, first_gain.astype(jnp.float32)).astype(jnp.bfloat16)
    query_rows = jnp.dot(normed, query_weight, preferred_element_type=jnp.float32).astype(
        jnp.bfloat16
    )
    key_rows = jnp.dot(normed, key_weight, preferred_element_type=jnp.float32).astype(jnp.bfloat16)
    value_rows = jnp.dot(normed, value_weight, preferred_element_type=jnp.float32).astype(
        jnp.bfloat16
    )
    context, log_totals = attend_forward(query_rows, key_rows, value_rows, allowed)
    context = context.astype(jnp.bfloat16)
    hidden_in = inputs + jnp.dot(context, output_weight, preferred_element_type=jnp.float32)
    second = layer_norm(hidden_in, second_gain.astype(jnp.float32)).astype(jnp.bfloat16)
    slot_of, token_of, filled = tables
    slot_rows = jnp.where(filled[:, None] == 1, second[token_of], jnp.zeros((), jnp.bfloat16))
    everyone = lax.all_gather(slot_rows, "expert", axis=0, tiled=True)
    grouped = everyone.reshape(-1, EXPERTS, MOST, width)
    before = jnp.einsum("demc,ecf->demf", grouped, weight_in, preferred_element_type=jnp.float32)
    activated = jax.nn.gelu(before, approximate=False).astype(jnp.bfloat16)
    partial_sums = jnp.einsum(
        "demf,efc->demc", activated, weight_out, preferred_element_type=jnp.float32
    )
    own_sums = lax.psum_scatter(
        partial_sums.reshape(-1, width).astype(jnp.bfloat16),
        "expert",
        scatter_dimension=0,
        tiled=True,
    ).astype(jnp.float32)
    outputs = hidden_in + own_sums[slot_of]
    kept = (
        inputs,
        normed,
        query_rows,
        key_rows,
        value_rows,
        log_totals,
        context,
        hidden_in,
        grouped,
        before,
        activated,
    )
    return (outputs, kept)


def layer_backward(grad_outputs, allowed, tables, attention, experts_full, kept):
    query_weight, key_weight, value_weight, output_weight, first_gain, second_gain = attention
    weight_in, weight_out = experts_full
    (
        inputs,
        normed,
        query_rows,
        key_rows,
        value_rows,
        log_totals,
        context,
        hidden_in,
        grouped,
        before,
        activated,
    ) = kept
    slot_of, token_of, filled = tables
    width = grad_outputs.shape[1]
    hidden_units = weight_in.shape[2]
    out_grad = grad_outputs.astype(jnp.bfloat16)
    slot_grads = jnp.where(filled[:, None] == 1, out_grad[token_of], jnp.zeros((), jnp.bfloat16))
    every_grad = lax.all_gather(slot_grads, "expert", axis=0, tiled=True).reshape(grouped.shape)
    active_grad = jnp.einsum(
        "demc,efc->demf", every_grad, weight_out, preferred_element_type=jnp.float32
    )
    _, slope_back = jax.vjp(partial(jax.nn.gelu, approximate=False), before)
    before_grad = slope_back(active_grad)[0].astype(jnp.bfloat16)
    expert_rows = weight_in.shape[1] // lax.axis_size("dp")
    in_term = jnp.einsum("demc,demf->cef", grouped, before_grad, preferred_element_type=jnp.float32)
    out_term = jnp.einsum(
        "demf,demc->cef", activated, every_grad, preferred_element_type=jnp.float32
    )
    expert_total = lax.psum_scatter(
        jnp.stack([in_term, out_term], 1).reshape(
            lax.axis_size("dp") * expert_rows, 2 * EXPERTS * hidden_units
        ),
        "dp",
        scatter_dimension=0,
        tiled=True,
    )
    expert_total = expert_total.reshape(expert_rows, 2, EXPERTS, hidden_units)
    in_weight_grad = jnp.transpose(expert_total[:, 0], (1, 0, 2))
    out_weight_grad = jnp.transpose(expert_total[:, 1], (1, 2, 0))
    input_part = jnp.einsum(
        "demf,ecf->demc", before_grad, weight_in, preferred_element_type=jnp.float32
    )
    slot_input = lax.psum_scatter(
        input_part.reshape(-1, width).astype(jnp.bfloat16),
        "expert",
        scatter_dimension=0,
        tiled=True,
    ).astype(jnp.float32)
    second_grad = slot_input[slot_of]
    _, second_back = jax.vjp(layer_norm, hidden_in, second_gain.astype(jnp.float32))
    hidden_norm_grad, second_gain_grad = second_back(second_grad)
    hidden_grad = grad_outputs + hidden_norm_grad
    branch_grad = hidden_grad.astype(jnp.bfloat16)
    context_grad = contract_cols(branch_grad, output_weight).astype(jnp.bfloat16)
    query_grad, key_grad, value_grad = attend_backward(
        query_rows, key_rows, value_rows, allowed, log_totals, context_grad
    )
    normed_grad = (
        contract_cols(query_grad, query_weight)
        + contract_cols(key_grad, key_weight)
        + contract_cols(value_grad, value_weight)
    )
    attention_total = lax.psum_scatter(
        jnp.concatenate(
            [
                contract_rows(normed, query_grad),
                contract_rows(normed, key_grad),
                contract_rows(normed, value_grad),
                contract_rows(context, branch_grad),
            ],
            1,
        ),
        ("dp", "expert"),
        scatter_dimension=0,
        tiled=True,
    )
    _, first_back = jax.vjp(layer_norm, inputs, first_gain.astype(jnp.float32))
    input_norm_grad, first_gain_grad = first_back(normed_grad)
    input_grad = hidden_grad + input_norm_grad
    gain_total = (
        lax.psum_scatter(first_gain_grad, ("dp", "expert"), scatter_dimension=0, tiled=True),
        lax.psum_scatter(second_gain_grad, ("dp", "expert"), scatter_dimension=0, tiled=True),
    )
    attention_part = (
        attention_total[:, 0:width],
        attention_total[:, width : 2 * width],
        attention_total[:, 2 * width : 3 * width],
        attention_total[:, 3 * width : 4 * width],
        gain_total[0],
        gain_total[1],
    )
    return (input_grad, attention_part, (in_weight_grad, out_weight_grad))


def on_device(
    tokens,
    groups,
    key_mask,
    routes,
    query_weight,
    key_weight,
    value_weight,
    output_weight,
    norm_first,
    norm_second,
    expert_in,
    expert_out,
    cotangent,
):
    allowed = allowed_pairs(groups[0], key_mask)
    tables = slot_tables(routes[:, 0])
    state = tokens.astype(jnp.float32)
    saved = []
    for layer_index in range(LAYERS):
        attention = (
            lax.all_gather(query_weight[layer_index], ("dp", "expert"), axis=0, tiled=True),
            lax.all_gather(key_weight[layer_index], ("dp", "expert"), axis=0, tiled=True),
            lax.all_gather(value_weight[layer_index], ("dp", "expert"), axis=0, tiled=True),
            lax.all_gather(output_weight[layer_index], ("dp", "expert"), axis=0, tiled=True),
            lax.all_gather(norm_first[layer_index], ("dp", "expert"), axis=0, tiled=True),
            lax.all_gather(norm_second[layer_index], ("dp", "expert"), axis=0, tiled=True),
        )
        experts_full = (
            lax.all_gather(expert_in[layer_index], "dp", axis=1, tiled=True),
            lax.all_gather(expert_out[layer_index], "dp", axis=2, tiled=True),
        )
        state, kept = layer_forward(state, allowed, tables, attention, experts_full)
        saved.append((attention, experts_full, kept))
    mixed = state.astype(jnp.bfloat16)
    grad_state = cotangent
    results = [None] * LAYERS
    for layer_index in reversed(range(LAYERS)):
        attention, experts_full, kept = saved[layer_index]
        attention = (
            lax.all_gather(query_weight[layer_index], ("dp", "expert"), axis=0, tiled=True),
            lax.all_gather(key_weight[layer_index], ("dp", "expert"), axis=0, tiled=True),
            lax.all_gather(value_weight[layer_index], ("dp", "expert"), axis=0, tiled=True),
            lax.all_gather(output_weight[layer_index], ("dp", "expert"), axis=0, tiled=True),
            lax.all_gather(norm_first[layer_index], ("dp", "expert"), axis=0, tiled=True),
            lax.all_gather(norm_second[layer_index], ("dp", "expert"), axis=0, tiled=True),
        )
        experts_full = (
            lax.all_gather(expert_in[layer_index], "dp", axis=1, tiled=True),
            lax.all_gather(expert_out[layer_index], "dp", axis=2, tiled=True),
        )
        grad_state, attention_part, expert_part = layer_backward(
            grad_state, allowed, tables, attention, experts_full, kept
        )
        results[layer_index] = (attention_part, expert_part)
    delta_query = jnp.stack([results[index][0][0] for index in range(LAYERS)])
    delta_key = jnp.stack([results[index][0][1] for index in range(LAYERS)])
    delta_value = jnp.stack([results[index][0][2] for index in range(LAYERS)])
    delta_output = jnp.stack([results[index][0][3] for index in range(LAYERS)])
    delta_first = jnp.stack([results[index][0][4] for index in range(LAYERS)])
    delta_second = jnp.stack([results[index][0][5] for index in range(LAYERS)])
    delta_in = jnp.stack([results[index][1][0] for index in range(LAYERS)])
    delta_out = jnp.stack([results[index][1][1] for index in range(LAYERS)])
    return (
        mixed,
        grad_state,
        delta_query,
        delta_key,
        delta_value,
        delta_output,
        delta_first,
        delta_second,
        delta_in,
        delta_out,
    )


def solution(mesh):
    placed = (
        P(("dp", "expert"), None),
        P(("dp", "expert"), None),
        P(("dp", "expert")),
        P(("dp", "expert"), None),
        P(None, ("dp", "expert"), None),
        P(None, ("dp", "expert"), None),
        P(None, ("dp", "expert"), None),
        P(None, ("dp", "expert"), None),
        P(None, ("dp", "expert")),
        P(None, ("dp", "expert")),
        P(None, None, "dp", "expert"),
        P(None, None, "expert", "dp"),
        P(("dp", "expert"), None),
    )
    return jax.shard_map(
        on_device,
        mesh=mesh,
        in_specs=placed,
        out_specs=(
            P(("dp", "expert"), None),
            P(("dp", "expert"), None),
            P(None, ("dp", "expert"), None),
            P(None, ("dp", "expert"), None),
            P(None, ("dp", "expert"), None),
            P(None, ("dp", "expert"), None),
            P(None, ("dp", "expert")),
            P(None, ("dp", "expert")),
            P(None, None, "dp", "expert"),
            P(None, None, "expert", "dp"),
        ),
        check_vma=False,
    )
```

profile of v0, /device:TPU:0, one launch (start us, length us, event | category | flops | bytes accessed | tf_op | source)
XLA Modules:
  0.0 1962.7 jit_solution(9064034768107004105)
XLA Ops:
  16.4 42.1 %all-reduce.9 = (bf16[768]{0:T(1024)(128)(2,1)S(1)}, bf16[768]{0:T(1024)(128)(2,1)S(1)}, bf16[768]{0:T(1024)(128)(2,1)}, bf16[768]{0:T(1024)(128)(2,1)}) all-reduce(bf16[768]{0:T(1024)(128)(2,1)S(1)} %dynamic-update-slice, bf16[768]{0:T(1024)(128)(2,1)S(1)} %dynamic-update-slice.1, ...), channel_id=2, replica_groups=mesh['dp'=8,'expert'=4] {'dp','expert'}, use_global_device_ids=true, to_apply=%add | all-reduce | flops 3072 | bytes 12288
  70.7 54.2 %all-gather.43.cloned.1.call-done = bf16[1,768,768]{2,1,0:T(8,128)(2,1)} async-done(((bf16[1,24,768]{2,1,0:T(8,128)(2,1)}), bf16[1,768,768]{2,1,0:T(8,128)(2,1)}) %all-gather.43.cloned.1.call-update) | async-done | bytes 1179664 | tf_op jit(solution)/shard_map/all_gather | solution.py:275
  126.9 54.5 %all-gather.41.cloned.1.call-done = bf16[1,768,768]{2,1,0:T(8,128)(2,1)} async-done(((bf16[1,24,768]{2,1,0:T(8,128)(2,1)}), bf16[1,768,768]{2,1,0:T(8,128)(2,1)}) %all-gather.41.cloned.1.call-update) | async-done | bytes 1179664 | tf_op jit(solution)/shard_map/all_gather | solution.py:274
  184.6 57.9 %while.56 = (s32[]{:T(128)}, bf16[12,384,64]{1,2,0:T(8,128)(2,1)S(1)}, f32[12,384]{1,0:T(8,128)}, s32[12]{0:T(128)}, bf16[384,768]{1,0:T(8,128)(2,1)S(1)}, /*ind...) while((s32[]{:T(128)}, ...), condition=%wide.region_5.6_spmd.clone, body=%wide.region_2.0_spmd.clone.sunk | while | flops 39517828 | bytes 2187971 | solution.py:82
  251.2 53.3 %all-gather.49.cloned.1.call-done = bf16[1,3,768,768]{3,2,1,0:T(8,128)(2,1)} async-done(((bf16[1,3,96,768]{3,2,1,0:T(8,128)(2,1)}), bf16[1,3,768,768]{3,2,1,0:T(8,128)(2,1)}) %all-gather.49.cloned.1.call-update) | async-done | bytes 3538960 | tf_op jit(solution)/shard_map/all_gather | solution.py:282
  304.6 26.2 %all-gather.33.cloned.1.call-done = bf16[1728,768]{1,0:T(8,128)(2,1)} async-done(((bf16[432,768]{1,0:T(8,128)(2,1)}), bf16[1728,768]{1,0:T(8,128)(2,1)}) %all-gather.33.cloned.1.call-update) | async-done | bytes 2654224 | tf_op jit(solution)/shard_map/all_gather | solution.py:125
  330.8 16.5 fusion.101
  347.3 51.5 %all-gather.51.cloned.1.call-done = bf16[1,3,768,768]{2,3,1,0:T(8,128)(2,1)} async-done(((bf16[1,3,768,96]{2,3,1,0:T(8,128)(2,1)}), bf16[1,3,768,768]{2,3,1,0:T(8,128)(2,1)}) %all-gather.51.cloned.1.call-update) | async-done | bytes 3538960 | tf_op jit(solution)/shard_map/all_gather | solution.py:283
  411.8 27.2 %reduce-scatter.13.cloned.1.call-done = bf16[432,768]{1,0:T(8,128)(2,1)} async-done(((bf16[1728,768]{1,0:T(8,128)(2,1)}), bf16[432,768]{1,0:T(8,128)(2,1)}) %reduce-scatter.13.cloned.1.call-update) | async-done | bytes 663568 | tf_op jit(solution)/shard_map/reduce_scatter | solution.py:132
  444.7 51.7 %all-gather.57.cloned.1.call-done = bf16[1,768,768]{2,1,0:T(8,128)(2,1)} async-done(((bf16[1,24,768]{2,1,0:T(8,128)(2,1)}), bf16[1,768,768]{2,1,0:T(8,128)(2,1)}) %all-gather.57.cloned.1.call-update) | async-done | bytes 1179664 | tf_op jit(solution)/shard_map/all_gather | solution.py:276
  499.2 54.0 %all-gather.55.cloned.1.call-done = bf16[1,768,768]{2,1,0:T(8,128)(2,1)} async-done(((bf16[1,24,768]{2,1,0:T(8,128)(2,1)}), bf16[1,768,768]{2,1,0:T(8,128)(2,1)}) %all-gather.55.cloned.1.call-update) | async-done | bytes 1179664 | tf_op jit(solution)/shard_map/all_gather | solution.py:275
  555.9 54.1 %all-gather.53.cloned.1.call-done = bf16[1,768,768]{2,1,0:T(8,128)(2,1)} async-done(((bf16[1,24,768]{2,1,0:T(8,128)(2,1)}), bf16[1,768,768]{2,1,0:T(8,128)(2,1)}) %all-gather.53.cloned.1.call-update) | async-done | bytes 1179664 | tf_op jit(solution)/shard_map/all_gather | solution.py:274
  614.8 78.2 %while.57 = (s32[]{:T(128)}, bf16[12,384,64]{1,2,0:T(8,128)(2,1)}, f32[12,384]{1,0:T(8,128)}, s32[12]{0:T(128)}, bf16[384,768]{1,0:T(8,128)(2,1)}, /*index=5*/bf...) while((s32[]{:T(128)}, bf16[12,384,64]{1,2,0:T(8,128)(2,1)}, ...), condition=%wide.region_19.20_spmd.clone, body=%wide.region_16.19_spmd.clone.sunk | while | flops 39517828 | bytes 2187455 | solution.py:82
  702.9 30.5 %all-gather.61.cloned.1.call-done = bf16[1,3,768,768]{3,2,1,0:T(8,128)(2,1)} async-done(((bf16[1,3,96,768]{3,2,1,0:T(8,128)(2,1)}), bf16[1,3,768,768]{3,2,1,0:T(8,128)(2,1)}) %all-gather.61.cloned.1.call-update) | async-done | bytes 3538960 | tf_op jit(solution)/shard_map/all_gather | solution.py:282
  733.4 26.3 %all-gather.35.cloned.1.call-done = bf16[1728,768]{1,0:T(8,128)(2,1)} async-done(((bf16[432,768]{1,0:T(8,128)(2,1)}), bf16[1728,768]{1,0:T(8,128)(2,1)}) %all-gather.35.cloned.1.call-update) | async-done | bytes 2654224 | tf_op jit(solution)/shard_map/all_gather | solution.py:125
  759.7 16.5 fusion.99
  776.3 51.0 %all-gather.63.cloned.1.call-done = bf16[1,3,768,768]{2,3,1,0:T(8,128)(2,1)} async-done(((bf16[1,3,768,96]{2,3,1,0:T(8,128)(2,1)}), bf16[1,3,768,768]{2,3,1,0:T(8,128)(2,1)}) %all-gather.63.cloned.1.call-update) | async-done | bytes 3538960 | tf_op jit(solution)/shard_map/all_gather | solution.py:283
  827.2 26.3 %all-gather.37.cloned.1.call-done = bf16[1728,768]{1,0:T(8,128)(2,1)} async-done(((bf16[432,768]{1,0:T(8,128)(2,1)}), bf16[1728,768]{1,0:T(8,128)(2,1)}) %all-gather.37.cloned.1.call-update) | async-done | bytes 2654224 | tf_op jit(solution)/shard_map/all_gather | solution.py:176
  874.2 27.8 %reduce-scatter.17.cloned.1.call-done = bf16[432,768]{1,0:T(8,128)(2,1)} async-done(((bf16[1728,768]{1,0:T(8,128)(2,1)}), bf16[432,768]{1,0:T(8,128)(2,1)}) %reduce-scatter.17.cloned.1.call-update) | async-done | bytes 663568 | tf_op jit(solution)/shard_map/reduce_scatter | solution.py:201
  908.3 31.0 %reduce-scatter.15.cloned.1.call-done = bf16[432,768]{1,0:T(8,128)(2,1)} async-done(((bf16[1728,768]{1,0:T(8,128)(2,1)}), bf16[432,768]{1,0:T(8,128)(2,1)}) %reduce-scatter.15.cloned.1.call-update) | async-done | bytes 663568 | tf_op jit(solution)/shard_map/reduce_scatter | solution.py:132
  951.8 146.1 %while.58 = (s32[]{:T(128)}, bf16[12,384,64]{1,2,0:T(8,128)(2,1)}, bf16[12,384,64]{1,2,0:T(8,128)(2,1)}, bf16[12,384,64]{1,2,0:T(8,128)(2,1)}, s32[12]{0:T(128)S...) while((s32[]{:T(128)}, bf16[12,384,64]{1,2,0:T(8,128)(2,1)}, ...), condition=%wide.region_28.29_spmd.clone, body=%wide.region_26.28_spmd.clone.sunk | while | flops 96337536 | bytes 5422857 | solution.py:103
  1111.3 25.7 %all-gather.39.cloned.1.call-done = bf16[1728,768]{1,0:T(8,128)(2,1)} async-done(((bf16[432,768]{1,0:T(8,128)(2,1)}), bf16[1728,768]{1,0:T(8,128)(2,1)}) %all-gather.39.cloned.1.call-update) | async-done | bytes 2654224 | tf_op jit(solution)/shard_map/all_gather | solution.py:176
  1160.0 9.8 copy.89
  1170.1 15.2 reduce-scatter.19.cloned.1.call-done
  1196.9 132.3 %while.59 = (s32[]{:T(128)}, bf16[12,384,64]{1,2,0:T(8,128)(2,1)S(1)}, bf16[12,384,64]{1,2,0:T(8,128)(2,1)}, bf16[12,384,64]{1,2,0:T(8,128)(2,1)S(1)}, s32[12]{0...) while((s32[]{:T(128)}, ...), condition=%wide.region_36.37_spmd.clone, body=%wide.region_34.36_spmd.clone.sunk | while | flops 96337536 | bytes 5422857 | solution.py:103
  1360.8 12.8 pad_maximum_fusion.1
  1373.7 15.6 copy.76
  1403.4 11.8 pad_maximum_fusion
  1415.2 15.4 copy.73
  1435.8 40.5 %all-reduce.8 = (f32[768]{0:T(1024)S(1)}, f32[768]{0:T(1024)S(1)}, f32[768]{0:T(1024)S(1)}, f32[768]{0:T(1024)S(1)}) all-reduce(f32[768]{0:T(1024)} %get-tuple-element.358, f32[768]{0:T(1024)S(1)} %get-tuple-element.360, f32[768]{0:T(1024)S(1)} %copy-done.62, ...), channel_id=25, replica_groups=mesh['dp'=8,'expert'=4] {'dp','expert'}, use_global_device_ids=true, to_apply=%region_44.45.clone | all-reduce | flops 3072 | bytes 24576
  1486.8 228.4 %reduce-scatter.23.cloned.1.call-done = f32[96,4608]{1,0:T(8,128)} async-done(((f32[768,4608]{1,0:T(8,128)}), f32[96,4608]{1,0:T(8,128)}) %reduce-scatter.23.cloned.1.call-update) | async-done | bytes 1769488 | tf_op jit(solution)/shard_map/reduce_scatter | solution.py:187
  1719.6 227.4 %reduce-scatter.21.cloned.1.call-done = f32[96,4608]{1,0:T(8,128)} async-done(((f32[768,4608]{1,0:T(8,128)}), f32[96,4608]{1,0:T(8,128)}) %reduce-scatter.21.cloned.1.call-update) | async-done | bytes 1769488 | tf_op jit(solution)/shard_map/reduce_scatter | solution.py:187
  (755 shorter events, 569.7 us)
Async XLA Ops:
  7.2 61.5 %all-gather.45.cloned.1.call-start = ((), (), s32[]{:S(2)}) async-start(), calls=%async_computation.20 | async-start | bytes 1216512 | tf_op jit(solution)/shard_map/all_gather | solution.py:276
  8.8 116.2 %all-gather.43.cloned.1.call-start = ((), (), s32[]{:S(2)}) async-start(), calls=%async_computation.19 | async-start | bytes 1216512 | tf_op jit(solution)/shard_map/all_gather | solution.py:275
  10.3 171.1 %all-gather.41.cloned.1.call-start = ((), (), s32[]{:S(2)}) async-start(), calls=%async_computation.18 | async-start | bytes 1216512 | tf_op jit(solution)/shard_map/all_gather | solution.py:274
  11.8 230.8 %all-gather.47.cloned.1.call-start = ((), (), s32[]{:S(2)}) async-start(), calls=%async_computation.21 | async-start | bytes 1216512 | tf_op jit(solution)/shard_map/all_gather | solution.py:277
  13.3 291.3 %all-gather.49.cloned.1.call-start = ((), (), s32[]{:S(2)}) async-start(), calls=%async_computation.22 | async-start | bytes 3981312 | tf_op jit(solution)/shard_map/all_gather | solution.py:282
  15.5 315.3 %all-gather.33.cloned.1.call-start = ((), (), s32[]{:S(2)}) async-start(), calls=%async_computation.8 | async-start | bytes 3317760 | tf_op jit(solution)/shard_map/all_gather | solution.py:125
  58.6 122.9 %copy-start.34 = (f32[768]{0:T(1024)}, f32[768]{0:T(1024)S(1)}, u32[]{:S(2)}) copy-start(f32[768]{0:T(1024)S(1)} %convert_element_type.296) | copy-start | bytes 9220
  60.3 185.9 %copy-start.40 = (f32[768]{0:T(1024)}, f32[768]{0:T(1024)S(1)}, u32[]{:S(2)}) copy-start(f32[768]{0:T(1024)S(1)} %convert_element_type.297) | copy-start | bytes 9220
  249.6 149.2 %all-gather.51.cloned.1.call-start = ((), (), s32[]{:S(2)}) async-start(), calls=%async_computation.23 | async-start | bytes 3981312 | tf_op jit(solution)/shard_map/all_gather | solution.py:283
  251.0 188.1 %reduce-scatter.13.cloned.1.call-start = ((), (), s32[]{:S(2)}) async-start(), calls=%async_computation.9 | async-start | bytes 3317760 | tf_op jit(solution)/shard_map/reduce_scatter | solution.py:132
  405.6 90.9 %all-gather.57.cloned.1.call-start = ((), (), s32[]{:S(2)}) async-start(), calls=%async_computation.26 | async-start | bytes 1216512 | tf_op jit(solution)/shard_map/all_gather | solution.py:276
  406.3 146.9 %all-gather.55.cloned.1.call-start = ((), (), s32[]{:S(2)}) async-start(), calls=%async_computation.25 | async-start | bytes 1216512 | tf_op jit(solution)/shard_map/all_gather | solution.py:275
  406.9 203.2 %all-gather.53.cloned.1.call-start = ((), (), s32[]{:S(2)}) async-start(), calls=%async_computation.24 | async-start | bytes 1216512 | tf_op jit(solution)/shard_map/all_gather | solution.py:274
  407.6 285.3 %all-gather.59.cloned.1.call-start = ((), (), s32[]{:S(2)}) async-start(), calls=%async_computation.27 | async-start | bytes 1216512 | tf_op jit(solution)/shard_map/all_gather | solution.py:277
  408.2 325.2 %all-gather.61.cloned.1.call-start = ((), (), s32[]{:S(2)}) async-start(), calls=%async_computation.28 | async-start | bytes 3981312 | tf_op jit(solution)/shard_map/all_gather | solution.py:282
  408.9 350.8 %all-gather.35.cloned.1.call-start = ((), (), s32[]{:S(2)}) async-start(), calls=%async_computation.10 | async-start | bytes 3317760 | tf_op jit(solution)/shard_map/all_gather | solution.py:125
  444.2 248.8 %copy-start.2 = (f32[384,768]{1,0:T(8,128)}, f32[384,768]{1,0:T(8,128)S(1)}, u32[]{:S(2)}) copy-start(f32[384,768]{1,0:T(8,128)S(1)} %get-tuple-element.463) | copy-start | bytes 3538948
  701.5 125.7 %all-gather.63.cloned.1.call-start = ((), (), s32[]{:S(2)}) async-start(), calls=%async_computation.29 | async-start | bytes 3981312 | tf_op jit(solution)/shard_map/all_gather | solution.py:283
  702.1 151.5 %all-gather.37.cloned.1.call-start = ((), (), s32[]{:S(2)}) async-start(), calls=%async_computation.12 | async-start | bytes 3317760 | tf_op jit(solution)/shard_map/all_gather | solution.py:176
  702.7 199.3 %reduce-scatter.17.cloned.1.call-start = ((), (), s32[]{:S(2)}) async-start(), calls=%async_computation.13 | async-start | bytes 3317760 | tf_op jit(solution)/shard_map/reduce_scatter | solution.py:201
  866.9 72.4 %reduce-scatter.15.cloned.1.call-start = ((), (), s32[]{:S(2)}) async-start(), calls=%async_computation.11 | async-start | bytes 3317760 | tf_op jit(solution)/shard_map/reduce_scatter | solution.py:132
  873.7 263.3 %all-gather.39.cloned.1.call-start = ((), (), s32[]{:S(2)}) async-start(), calls=%async_computation.14 | async-start | bytes 3317760 | tf_op jit(solution)/shard_map/all_gather | solution.py:176
  947.6 207.5 %copy-start.4 = (f32[384,768]{1,0:T(8,128)}, f32[384,768]{1,0:T(8,128)S(1)}, u32[]{:S(2)}) copy-start(f32[384,768]{1,0:T(8,128)S(1)} %add_add_fusion.7) | copy-start | bytes 3538948
  1111.1 74.3 %reduce-scatter.19.cloned.1.call-start = ((), (), s32[]{:S(2)}) async-start(), calls=%async_computation.15 | async-start | bytes 3317760 | tf_op jit(solution)/shard_map/reduce_scatter | solution.py:201
  1150.3 328.8 %reduce-scatter.27.cloned.1.call-start = ((), (), s32[]{:S(2)}) async-start(), calls=%async_computation.31 | async-start | bytes 9732096
  1169.8 313.2 %reduce-scatter.25.cloned.1.call-start = ((), (), s32[]{:S(2)}) async-start(), calls=%async_computation.30 | async-start | bytes 9732096
  1196.9 132.4 %copy-start.1 = (bf16[384,768]{1,0:T(8,128)(2,1)S(1)}, bf16[384,768]{1,0:T(8,128)(2,1)}, u32[]{:S(2)}) copy-start(bf16[384,768]{1,0:T(8,128)(2,1)} %param.21) | copy-start | bytes 1769476
  1196.9 132.4 %copy-start.35 = (f32[768]{0:T(1024)S(1)}, f32[768]{0:T(1024)}, u32[]{:S(2)}) copy-start(f32[768]{0:T(1024)} %copy-done.34) | copy-start | bytes 9220
  1196.9 132.4 %copy-start.37 = (f32[384]{0:T(512)S(1)}, f32[384]{0:T(512)}, u32[]{:S(2)}) copy-start(f32[384]{0:T(512)} %copy-done.36) | copy-start | bytes 4612
  1196.9 132.4 %copy-start.39 = (f32[384]{0:T(512)S(1)}, f32[384]{0:T(512)}, u32[]{:S(2)}) copy-start(f32[384]{0:T(512)} %copy-done.38) | copy-start | bytes 4612
  1346.9 368.3 %reduce-scatter.23.cloned.1.call-start = ((), (), s32[]{:S(2)}) async-start(), calls=%async_computation.17 | async-start | bytes 15925248 | tf_op jit(solution)/shard_map/reduce_scatter | solution.py:187
  1389.3 557.8 %reduce-scatter.21.cloned.1.call-start = ((), (), s32[]{:S(2)}) async-start(), calls=%async_computation.16 | async-start | bytes 15925248 | tf_op jit(solution)/shard_map/reduce_scatter | solution.py:187
  (75 other events, 1069.9 us)
Sparse Core Ops, SparseCore 0:
  11.5 56.7 all-gather.44
  71.8 53.1 all-gather.42
  128.4 52.9 all-gather.40
  184.7 53.0 all-gather.46
  240.4 64.1 all-gather.48
  306.6 24.2 all-gather.32
  333.6 65.1 all-gather.50
  405.7 33.3 reduce-scatter.12
  442.4 54.0 all-gather.56
  500.2 52.9 all-gather.54
  557.1 52.9 all-gather.52
  613.2 53.0 all-gather.58
  669.3 64.0 all-gather.60
  735.5 24.2 all-gather.34
  762.0 65.1 all-gather.62
  829.3 24.2 all-gather.36
  867.0 34.8 reduce-scatter.16
  904.4 34.8 reduce-scatter.14
  1111.2 25.7 all-gather.38
  1150.4 34.8 reduce-scatter.18
  1191.2 135.6 reduce-scatter.26
  1347.0 135.9 reduce-scatter.24
  1486.7 228.4 reduce-scatter.22
  1718.7 228.2 reduce-scatter.20
where the time goes:
time: 1980 us; the launch traced here: 1960 us
  waiting for transfers between devices  1120 us (57%)
  matrix products  369 us (19%)
  local copies, waits for them, and re-layouts  220 us (11%)
  blocking collectives  82.7 us (4%)
  loops' own time  79.3 us (4%)
  other arithmetic  70.6 us (4%)
    reduce_scatter x2, waiting for transfers between devices, layer_backward(): lax.psum_scatter(jnp.stack([in_term, out_term], 1).reshape(lax.axis_size(...  456 us
    all_gather x2, waiting for transfers between devices, on_device(): lax.all_gather(query_weight[layer_index], ('dp', 'expert'), axis=0, tiled...  109 us
    all_gather x2, waiting for transfers between devices, on_device(): lax.all_gather(key_weight[layer_index], ('dp', 'expert'), axis=0, tiled=T...  108 us
    dot_general x80, matrix products, contract_cols(): lax.dot_general(left, right, (((1,), (1,)), ((), ())), preferred_element_...  106 us
    all_gather x2, waiting for transfers between devices, on_device(): lax.all_gather(expert_out[layer_index], 'dp', axis=2, tiled=True)  102 us
    dot_general x56, matrix products, contract_rows(): lax.dot_general(left, right, (((0,), (0,)), ((), ())), preferred_element_...  89.6 us
    all_gather x2, waiting for transfers between devices, on_device(): lax.all_gather(expert_in[layer_index], 'dp', axis=1, tiled=True)  83.8 us
    unnamed x2, blocking collectives  82.7 us
  transfers between devices with their start and end apart: 24, of which 20 were waited for; matrix products, arithmetic and copies ran while one was open for 24% of the time, Pallas kernels for 0%

commit v1 on v0

--- a/solution.py
+++ b/solution.py
@@ -11,6 +11,19 @@
 MOST = 144
 epsilon = 1e-05
 score_scale = 0.125
+
+
+def order_links_on_mesh(in_dim, mesh_ax, vector):
+    dev_n = lax.psum(1, axis_name=mesh_ax)
+    v_next = sorted(((idx, (idx + 1) % dev_n) for idx in range(dev_n)))
+    w_next = vector
+    by_place = [w_next]
+    for ix in [*range(1, dev_n)]:
+        w_next = lax.ppermute(w_next, axis_name=mesh_ax, perm=v_next)
+        by_place.insert(0, w_next)
+    main = jnp.concatenate(by_place, axis=in_dim)
+    latest = lax.axis_index(mesh_ax) + 1
+    return jnp.roll(main, latest * vector.shape[in_dim], axis=in_dim)
 
 
 def layer_norm(values, gain_vector):
@@ -122,7 +135,7 @@
     second = layer_norm(hidden_in, second_gain.astype(jnp.float32)).astype(jnp.bfloat16)
     slot_of, token_of, filled = tables
     slot_rows = jnp.where(filled[:, None] == 1, second[token_of], jnp.zeros((), jnp.bfloat16))
-    everyone = lax.all_gather(slot_rows, "expert", axis=0, tiled=True)
+    everyone = order_links_on_mesh(0, "expert", slot_rows)
     grouped = everyone.reshape(-1, EXPERTS, MOST, width)
     before = jnp.einsum("demc,ecf->demf", grouped, weight_in, preferred_element_type=jnp.float32)
     activated = jax.nn.gelu(before, approximate=False).astype(jnp.bfloat16)

time: 1980 us -> 1920 us (0.970)
  waiting for transfers between devices: 1120 us -> 1020 us
  other arithmetic: 70.6 us -> 106 us
    all_gather x2, waiting for transfers between devices: 83.8 us -> 5.79 us  [on_device(): lax.all_gather(expert_in[layer_index], 'dp', axis=1, tiled=True)]
    ppermute x0 -> x6, waiting for transfers between devices: none -> 57.9 us  [order_links_on_mesh(): w_next = lax.ppermute(w_next, axis_name=mesh_ax, perm=v_next)]
    all_gather x2 -> x0, waiting for transfers between devices: 52.6 us -> none  [layer_forward(): everyone = lax.all_gather(slot_rows, 'expert', axis=0, tiled=True)]
    concatenate x0 -> x2, other arithmetic: none -> 36.1 us  [order_links_on_mesh(): return jnp.roll(main, latest * vector.shape[in_dim], axis=in_dim)]
  transfers between devices with their start and end apart: 24 -> 28, of which waited for: 20 -> 23; matrix products, arithmetic and copies ran while one was open for 24% -> 27% of each run, Pallas kernels for 0% -> 0%
where the time goes in v1:
time: 1920 us; the launch traced here: 1900 us
  waiting for transfers between devices  1020 us (53%)
  matrix products  369 us (19%)
  local copies, waits for them, and re-layouts  220 us (11%)
  other arithmetic  106 us (6%)
  blocking collectives  82.8 us (4%)
  loops' own time  79.4 us (4%)
    reduce_scatter x2, waiting for transfers between devices, layer_backward(): lax.psum_scatter(jnp.stack([in_term, out_term], 1).reshape(lax.axis_size(...  456 us
    all_gather x2, waiting for transfers between devices, on_device(): lax.all_gather(query_weight[layer_index], ('dp', 'expert'), axis=0, tiled...  109 us
    all_gather x2, waiting for transfers between devices, on_device(): lax.all_gather(key_weight[layer_index], ('dp', 'expert'), axis=0, tiled=T...  108 us
    dot_general x80, matrix products, contract_cols(): lax.dot_general(left, right, (((1,), (1,)), ((), ())), preferred_element_...  106 us
    dot_general x56, matrix products, contract_rows(): lax.dot_general(left, right, (((0,), (0,)), ((), ())), preferred_element_...  89.5 us
    all_gather x2, waiting for transfers between devices, on_device(): lax.all_gather(expert_out[layer_index], 'dp', axis=2, tiled=True)  83.1 us
    unnamed x2, blocking collectives  82.8 us
    another operation x2, loops' own time, attend_backward(): parts = lax.map(one_head, jnp.arange(HEADS, dtype=jnp.int32))  63.2 us
  transfers between devices with their start and end apart: 28, of which 23 were waited for; matrix products, arithmetic and copies ran while one was open for 27% of the time, Pallas kernels for 0%

profile of v1, /device:TPU:0, one launch (start us, length us, event | category | flops | bytes accessed | tf_op | source)
XLA Modules:
  0.0 1899.0 jit_solution(1908586595621498170)
XLA Ops:
  16.4 42.2 %all-reduce.9 = (bf16[768]{0:T(1024)(128)(2,1)S(1)}, bf16[768]{0:T(1024)(128)(2,1)S(1)}, bf16[768]{0:T(1024)(128)(2,1)}, bf16[768]{0:T(1024)(128)(2,1)}) all-reduce(bf16[768]{0:T(1024)(128)(2,1)S(1)} %dynamic-update-slice, bf16[768]{0:T(1024)(128)(2,1)S(1)} %dynamic-update-slice.1, ...), channel_id=2, replica_groups=mesh['dp'=8,'expert'=4] {'dp','expert'}, use_global_device_ids=true, to_apply=%add | all-reduce | flops 3072 | bytes 12288
  70.7 54.2 %all-gather.37.cloned.1.call-done = bf16[1,768,768]{2,1,0:T(8,128)(2,1)} async-done(((bf16[1,24,768]{2,1,0:T(8,128)(2,1)}), bf16[1,768,768]{2,1,0:T(8,128)(2,1)}) %all-gather.37.cloned.1.call-update) | async-done | bytes 1179664 | tf_op jit(solution)/shard_map/all_gather | solution.py:288
  126.9 54.5 %all-gather.35.cloned.1.call-done = bf16[1,768,768]{2,1,0:T(8,128)(2,1)} async-done(((bf16[1,24,768]{2,1,0:T(8,128)(2,1)}), bf16[1,768,768]{2,1,0:T(8,128)(2,1)}) %all-gather.35.cloned.1.call-update) | async-done | bytes 1179664 | tf_op jit(solution)/shard_map/all_gather | solution.py:287
  184.6 57.7 %while.56 = (s32[]{:T(128)}, bf16[12,384,64]{1,2,0:T(8,128)(2,1)S(1)}, f32[12,384]{1,0:T(8,128)}, s32[12]{0:T(128)}, bf16[384,768]{1,0:T(8,128)(2,1)S(1)}, /*ind...) while((s32[]{:T(128)}, ...), condition=%wide.region_5.6_spmd.clone, body=%wide.region_2.0_spmd.clone.sunk | while | flops 39517828 | bytes 2187971 | solution.py:95
  258.7 10.1 collective-permute-done.1
  269.0 10.2 collective-permute-done.2
  279.2 19.6 %fusion.152 = bf16[1728,768]{1,0:T(8,128)(2,1)} fusion(s32[]{:T(128)S(6)} %select_n.98, bf16[432,768]{1,0:T(8,128)(2,1)} %collective-permute-done.2, bf16[432,768]{1,0:T(8,128)(2,1)S(1)} %collective-permute-done.1, bf16[432,768]{1,0:T(8,128)(2,1)S(1)} %collective-permute-done, bf16[432,768]{1,0:T(8,128)(2,1)S(1)} %broadcast_select_fusion.3), kind=kLoop, calls=%fused_computation.228 | loop fusion | flops 21233664 | bytes 5308420 | tf_op jit(solution)/shard_map/jit(_roll_dynamic)/concatenate | solution.py:26
  304.6 16.9 fusion.101
  321.5 49.4 %all-gather.45.cloned.1.call-done = bf16[1,3,768,768]{2,3,1,0:T(8,128)(2,1)} async-done(((bf16[1,3,768,96]{2,3,1,0:T(8,128)(2,1)}), bf16[1,3,768,768]{2,3,1,0:T(8,128)(2,1)}) %all-gather.45.cloned.1.call-update) | async-done | bytes 3538960 | tf_op jit(solution)/shard_map/all_gather | solution.py:296
  384.9 26.5 %reduce-scatter.13.cloned.1.call-done = bf16[432,768]{1,0:T(8,128)(2,1)} async-done(((bf16[1728,768]{1,0:T(8,128)(2,1)}), bf16[432,768]{1,0:T(8,128)(2,1)}) %reduce-scatter.13.cloned.1.call-update) | async-done | bytes 663568 | tf_op jit(solution)/shard_map/reduce_scatter | solution.py:145
  417.0 51.7 %all-gather.51.cloned.1.call-done = bf16[1,768,768]{2,1,0:T(8,128)(2,1)} async-done(((bf16[1,24,768]{2,1,0:T(8,128)(2,1)}), bf16[1,768,768]{2,1,0:T(8,128)(2,1)}) %all-gather.51.cloned.1.call-update) | async-done | bytes 1179664 | tf_op jit(solution)/shard_map/all_gather | solution.py:289
  471.4 54.2 %all-gather.49.cloned.1.call-done = bf16[1,768,768]{2,1,0:T(8,128)(2,1)} async-done(((bf16[1,24,768]{2,1,0:T(8,128)(2,1)}), bf16[1,768,768]{2,1,0:T(8,128)(2,1)}) %all-gather.49.cloned.1.call-update) | async-done | bytes 1179664 | tf_op jit(solution)/shard_map/all_gather | solution.py:288
  528.3 54.0 %all-gather.47.cloned.1.call-done = bf16[1,768,768]{2,1,0:T(8,128)(2,1)} async-done(((bf16[1,24,768]{2,1,0:T(8,128)(2,1)}), bf16[1,768,768]{2,1,0:T(8,128)(2,1)}) %all-gather.47.cloned.1.call-update) | async-done | bytes 1179664 | tf_op jit(solution)/shard_map/all_gather | solution.py:287
  587.1 78.2 %while.57 = (s32[]{:T(128)}, bf16[12,384,64]{1,2,0:T(8,128)(2,1)}, f32[12,384]{1,0:T(8,128)}, s32[12]{0:T(128)}, bf16[384,768]{1,0:T(8,128)(2,1)}, /*index=5*/bf...) while((s32[]{:T(128)}, bf16[12,384,64]{1,2,0:T(8,128)(2,1)}, ...), condition=%wide.region_19.21_spmd.clone, body=%wide.region_16.20_spmd.clone.sunk | while | flops 39517828 | bytes 2187455 | solution.py:95
  694.8 10.1 collective-permute-done.5
  704.9 16.5 fusion.145
  721.4 16.7 fusion.99
  738.2 33.7 %all-gather.57.cloned.1.call-done = bf16[1,3,768,768]{2,3,1,0:T(8,128)(2,1)} async-done(((bf16[1,3,768,96]{2,3,1,0:T(8,128)(2,1)}), bf16[1,3,768,768]{2,3,1,0:T(8,128)(2,1)}) %all-gather.57.cloned.1.call-update) | async-done | bytes 3538960 | tf_op jit(solution)/shard_map/all_gather | solution.py:296
  778.7 19.5 %all-gather.31.cloned.1.call-done = bf16[1728,768]{1,0:T(8,128)(2,1)} async-done(((bf16[432,768]{1,0:T(8,128)(2,1)}), bf16[1728,768]{1,0:T(8,128)(2,1)}) %all-gather.31.cloned.1.call-update) | async-done | bytes 2654224 | tf_op jit(solution)/shard_map/all_gather | solution.py:189
  811.4 24.2 %reduce-scatter.15.cloned.1.call-done = bf16[432,768]{1,0:T(8,128)(2,1)} async-done(((bf16[1728,768]{1,0:T(8,128)(2,1)}), bf16[432,768]{1,0:T(8,128)(2,1)}) %reduce-scatter.15.cloned.1.call-update) | async-done | bytes 663568 | tf_op jit(solution)/shard_map/reduce_scatter | solution.py:145
  839.5 33.4 %reduce-scatter.17.cloned.1.call-done = bf16[432,768]{1,0:T(8,128)(2,1)} async-done(((bf16[1728,768]{1,0:T(8,128)(2,1)}), bf16[432,768]{1,0:T(8,128)(2,1)}) %reduce-scatter.17.cloned.1.call-update) | async-done | bytes 663568 | tf_op jit(solution)/shard_map/reduce_scatter | solution.py:214
  887.5 146.0 %while.58 = (s32[]{:T(128)}, bf16[12,384,64]{1,2,0:T(8,128)(2,1)}, bf16[12,384,64]{1,2,0:T(8,128)(2,1)}, bf16[12,384,64]{1,2,0:T(8,128)(2,1)}, s32[12]{0:T(128)S...) while((s32[]{:T(128)}, bf16[12,384,64]{1,2,0:T(8,128)(2,1)}, ...), condition=%wide.region_28.30_spmd.clone, body=%wide.region_26.29_spmd.clone.sunk | while | flops 96337536 | bytes 5422857 | solution.py:116
  1047.3 25.4 %all-gather.33.cloned.1.call-done = bf16[1728,768]{1,0:T(8,128)(2,1)} async-done(((bf16[432,768]{1,0:T(8,128)(2,1)}), bf16[1728,768]{1,0:T(8,128)(2,1)}) %all-gather.33.cloned.1.call-update) | async-done | bytes 2654224 | tf_op jit(solution)/shard_map/all_gather | solution.py:189
  1105.8 15.3 reduce-scatter.19.cloned.1.call-done
  1132.8 132.3 %while.59 = (s32[]{:T(128)}, bf16[12,384,64]{1,2,0:T(8,128)(2,1)S(1)}, bf16[12,384,64]{1,2,0:T(8,128)(2,1)}, bf16[12,384,64]{1,2,0:T(8,128)(2,1)S(1)}, s32[12]{0...) while((s32[]{:T(128)}, ...), condition=%wide.region_36.38_spmd.clone, body=%wide.region_34.37_spmd.clone.sunk | while | flops 96337536 | bytes 5422857 | solution.py:116
  1296.7 12.8 pad_maximum_fusion.1
  1309.5 15.6 copy.76
  1339.0 11.9 pad_maximum_fusion
  1350.9 15.3 copy.73
  1371.4 40.7 %all-reduce.8 = (f32[768]{0:T(1024)S(1)}, f32[768]{0:T(1024)S(1)}, f32[768]{0:T(1024)S(1)}, f32[768]{0:T(1024)S(1)}) all-reduce(f32[768]{0:T(1024)} %get-tuple-element.359, f32[768]{0:T(1024)S(1)} %get-tuple-element.361, f32[768]{0:T(1024)S(1)} %copy-done.65, ...), channel_id=25, replica_groups=mesh['dp'=8,'expert'=4] {'dp','expert'}, use_global_device_ids=true, to_apply=%region_44.46.clone | all-reduce | flops 3072 | bytes 24576
  1423.0 228.1 %reduce-scatter.23.cloned.1.call-done = f32[96,4608]{1,0:T(8,128)} async-done(((f32[768,4608]{1,0:T(8,128)}), f32[96,4608]{1,0:T(8,128)}) %reduce-scatter.23.cloned.1.call-update) | async-done | bytes 1769488 | tf_op jit(solution)/shard_map/reduce_scatter | solution.py:200
  1655.5 227.5 %reduce-scatter.21.cloned.1.call-done = f32[96,4608]{1,0:T(8,128)} async-done(((f32[768,4608]{1,0:T(8,128)}), f32[96,4608]{1,0:T(8,128)}) %reduce-scatter.21.cloned.1.call-update) | async-done | bytes 1769488 | tf_op jit(solution)/shard_map/reduce_scatter | solution.py:200
  (765 shorter events, 613.3 us)
Async XLA Ops:
  7.2 61.5 %all-gather.39.cloned.1.call-start = ((), (), s32[]{:S(2)}) async-start(), calls=%async_computation.18 | async-start | bytes 1216512 | tf_op jit(solution)/shard_map/all_gather | solution.py:289
  8.8 116.2 %all-gather.37.cloned.1.call-start = ((), (), s32[]{:S(2)}) async-start(), calls=%async_computation.17 | async-start | bytes 1216512 | tf_op jit(solution)/shard_map/all_gather | solution.py:288
  10.3 171.1 %all-gather.35.cloned.1.call-start = ((), (), s32[]{:S(2)}) async-start(), calls=%async_computation.16 | async-start | bytes 1216512 | tf_op jit(solution)/shard_map/all_gather | solution.py:287
  11.8 230.6 %all-gather.41.cloned.1.call-start = ((), (), s32[]{:S(2)}) async-start(), calls=%async_computation.19 | async-start | bytes 1216512 | tf_op jit(solution)/shard_map/all_gather | solution.py:290
  13.3 291.3 %all-gather.43.cloned.1.call-start = ((), (), s32[]{:S(2)}) async-start(), calls=%async_computation.20 | async-start | bytes 3981312 | tf_op jit(solution)/shard_map/all_gather | solution.py:295
  15.5 355.5 %all-gather.45.cloned.1.call-start = ((), (), s32[]{:S(2)}) async-start(), calls=%async_computation.21 | async-start | bytes 3981312 | tf_op jit(solution)/shard_map/all_gather | solution.py:296
  60.3 185.7 %copy-start.43 = (f32[768]{0:T(1024)}, f32[768]{0:T(1024)S(1)}, u32[]{:S(2)}) copy-start(f32[768]{0:T(1024)S(1)} %convert_element_type.297) | copy-start | bytes 9220
  248.6 10.1 collective-permute-start
  251.0 160.3 %reduce-scatter.13.cloned.1.call-start = ((), (), s32[]{:S(2)}) async-start(), calls=%async_computation.8 | async-start | bytes 3317760 | tf_op jit(solution)/shard_map/reduce_scatter | solution.py:145
  258.7 10.1 collective-permute-start.1
  268.8 10.4 collective-permute-start.2
  377.8 90.9 %all-gather.51.cloned.1.call-start = ((), (), s32[]{:S(2)}) async-start(), calls=%async_computation.24 | async-start | bytes 1216512 | tf_op jit(solution)/shard_map/all_gather | solution.py:289
  378.6 147.0 %all-gather.49.cloned.1.call-start = ((), (), s32[]{:S(2)}) async-start(), calls=%async_computation.23 | async-start | bytes 1216512 | tf_op jit(solution)/shard_map/all_gather | solution.py:288
  379.3 203.0 %all-gather.47.cloned.1.call-start = ((), (), s32[]{:S(2)}) async-start(), calls=%async_computation.22 | async-start | bytes 1216512 | tf_op jit(solution)/shard_map/all_gather | solution.py:287
  379.9 285.3 %all-gather.53.cloned.1.call-start = ((), (), s32[]{:S(2)}) async-start(), calls=%async_computation.25 | async-start | bytes 1216512 | tf_op jit(solution)/shard_map/all_gather | solution.py:290
  380.6 340.8 %all-gather.55.cloned.1.call-start = ((), (), s32[]{:S(2)}) async-start(), calls=%async_computation.26 | async-start | bytes 3981312 | tf_op jit(solution)/shard_map/all_gather | solution.py:295
  381.2 390.6 %all-gather.57.cloned.1.call-start = ((), (), s32[]{:S(2)}) async-start(), calls=%async_computation.27 | async-start | bytes 3981312 | tf_op jit(solution)/shard_map/all_gather | solution.py:296
  382.0 416.2 %all-gather.31.cloned.1.call-start = ((), (), s32[]{:S(2)}) async-start(), calls=%async_computation.10 | async-start | bytes 3317760 | tf_op jit(solution)/shard_map/all_gather | solution.py:189
  416.5 248.8 %copy-start.2 = (f32[384,768]{1,0:T(8,128)}, f32[384,768]{1,0:T(8,128)S(1)}, u32[]{:S(2)}) copy-start(f32[384,768]{1,0:T(8,128)S(1)} %get-tuple-element.464) | copy-start | bytes 3538948
  674.4 10.1 collective-permute-start.3
  684.5 10.3 collective-permute-start.4
  694.7 10.2 collective-permute-start.5
  694.8 140.8 %reduce-scatter.15.cloned.1.call-start = ((), (), s32[]{:S(2)}) async-start(), calls=%async_computation.9 | async-start | bytes 3317760 | tf_op jit(solution)/shard_map/reduce_scatter | solution.py:145
  778.6 94.3 %reduce-scatter.17.cloned.1.call-start = ((), (), s32[]{:S(2)}) async-start(), calls=%async_computation.11 | async-start | bytes 3317760 | tf_op jit(solution)/shard_map/reduce_scatter | solution.py:214
  811.4 261.3 %all-gather.33.cloned.1.call-start = ((), (), s32[]{:S(2)}) async-start(), calls=%async_computation.12 | async-start | bytes 3317760 | tf_op jit(solution)/shard_map/all_gather | solution.py:189
  883.4 207.4 %copy-start.4 = (f32[384,768]{1,0:T(8,128)}, f32[384,768]{1,0:T(8,128)S(1)}, u32[]{:S(2)}) copy-start(f32[384,768]{1,0:T(8,128)S(1)} %add_add_fusion.7) | copy-start | bytes 3538948
  1046.8 74.2 %reduce-scatter.19.cloned.1.call-start = ((), (), s32[]{:S(2)}) async-start(), calls=%async_computation.13 | async-start | bytes 3317760 | tf_op jit(solution)/shard_map/reduce_scatter | solution.py:214
  1086.0 328.8 %reduce-scatter.27.cloned.1.call-start = ((), (), s32[]{:S(2)}) async-start(), calls=%async_computation.29 | async-start | bytes 9732096
  1105.5 313.7 %reduce-scatter.25.cloned.1.call-start = ((), (), s32[]{:S(2)}) async-start(), calls=%async_computation.28 | async-start | bytes 9732096
  1132.7 132.4 %copy-start.1 = (bf16[384,768]{1,0:T(8,128)(2,1)S(1)}, bf16[384,768]{1,0:T(8,128)(2,1)}, u32[]{:S(2)}) copy-start(bf16[384,768]{1,0:T(8,128)(2,1)} %param.23) | copy-start | bytes 1769476
  1282.8 368.3 %reduce-scatter.23.cloned.1.call-start = ((), (), s32[]{:S(2)}) async-start(), calls=%async_computation.15 | async-start | bytes 15925248 | tf_op jit(solution)/shard_map/reduce_scatter | solution.py:200
  1325.1 557.9 %reduce-scatter.21.cloned.1.call-start = ((), (), s32[]{:S(2)}) async-start(), calls=%async_computation.14 | async-start | bytes 15925248 | tf_op jit(solution)/shard_map/reduce_scatter | solution.py:200
  (80 other events, 1604.1 us)
Sparse Core Ops, SparseCore 0:
  11.5 56.7 all-gather.38
  71.8 53.0 all-gather.36
  128.4 52.9 all-gather.34
  184.8 53.0 all-gather.40
  240.5 64.0 all-gather.42
  307.2 63.6 all-gather.44
  378.0 33.3 reduce-scatter.12
  414.6 54.0 all-gather.50
  472.6 52.9 all-gather.48
  529.3 52.9 all-gather.46
  585.6 52.9 all-gather.52
  641.5 64.0 all-gather.54
  708.1 63.6 all-gather.56
  773.9 24.2 all-gather.30
  800.7 34.8 reduce-scatter.14
  838.0 34.8 reduce-scatter.16
  1046.9 25.7 all-gather.32
  1086.1 34.8 reduce-scatter.18
  1126.9 135.5 reduce-scatter.26
  1282.9 136.2 reduce-scatter.24
  1422.9 228.1 reduce-scatter.22
  1654.7 228.2 reduce-scatter.20
